TPU v7x, 32 devices: a whole 2x2x4 slice. The times are simulated.
32 devices in a mesh: expert: 4 (over y, core), shard: 8 (over z, x).
Axes of the slice: x: 2, y: 2, z: 4, core: 2. Of those that a mesh axis runs over, the one named last changes fastest.
Arguments:
- tokens: bfloat16 [8192, 1536], P(('expert', 'shard')), may hold values from -6 to 6
- lengths: int32 [32], P(('expert', 'shard')), may hold values from 64 to 256, as said below
- routes: int32 [8192, 8], P(('expert', 'shard')), may hold values from 0 to 19, all different within a row; in each aligned block of 256 rows (0 to 255, 256 to 511, ...) at most 104 rows name the same one
- cotangent: bfloat16 [8192, 1536], P(('expert', 'shard')), may hold values from -6 to 6
- first_gain: bfloat16 [1536], P('shard'), may hold values from 0.5 to 1.5
- query_weight: bfloat16 [1536, 1536], P('shard'), may hold values from -0.15625 to 0.15625
- key_matrix: bfloat16 [1536, 512], P('shard'), may hold values from -0.15625 to 0.15625
- value_matrix: bfloat16 [1536, 512], P('shard'), may hold values from -0.15625 to 0.15625
- output_weight: bfloat16 [1536, 1536], P('shard'), may hold values from -1.25 to 1.25
- second_gain: bfloat16 [1536], P('shard'), may hold values from 0.5 to 1.5
- router_weight: bfloat16 [1536, 20], P('shard'), may hold values from -0.078125 to 0.078125
- gate_up_weight: bfloat16 [1536, 20, 1024], P('shard', 'expert'), may hold values from -0.15625 to 0.15625
- down_weight: bfloat16 [1536, 20, 512], P('shard', 'expert'), may hold values from -1 to 1
Outputs:
- layer_out: bfloat16 [8192, 1536], P(('expert', 'shard'))
- tokens_grad: float32 [8192, 1536], P(('expert', 'shard'))
- first_gain_grad: float32 [1536], P('shard')
- query_grad: float32 [1536, 1536], P('shard')
- key_grad: float32 [1536, 512], P('shard')
- value_grad: float32 [1536, 512], P('shard')
- output_grad: float32 [1536, 1536], P('shard')
- second_gain_grad: float32 [1536], P('shard')
- router_grad: float32 [1536, 20], P('shard')
- gate_up_grad: float32 [1536, 20, 1024], P('shard', 'expert')
- down_grad: float32 [1536, 20, 512], P('shard', 'expert')
Inputs may be any that keep to these rules, and one draw needn't show every extreme that they name: `lengths`: some sequence has 256 valid tokens and some 256 // 4. `routes`: each row names 8 different experts; among the 256 rows of one sequence no expert is named more than 104 times, a bound that some block reaches.
All inputs are finite; a program needn't handle non-finite values.
Results may differ from a plain program's by a relative error of at most 0.02.
Values may be sent and summed in bfloat16 or wider, within the bound.
A program may use at most 320 MiB of HBM per device.

v0:
```python
import jax
import jax.numpy as jnp
from jax import lax
from jax.sharding import PartitionSpec as P

HEAD_DIM = 64
norm_eps = 1e-06


def product(form, left, right):
    return jnp.einsum(form, left, right, preferred_element_type=jnp.float32)


def rope_tables(row_count, head_width):
    half_width = head_width // 2
    frequency = 10000.0 ** (-(jnp.arange(half_width, dtype=jnp.float32) * (2.0 / head_width)))
    angles = jnp.arange(row_count, dtype=jnp.float32)[:, None] * frequency[None, :]
    return (jnp.cos(angles)[:, None, :], jnp.sin(angles)[:, None, :])


def rotate(values_in, cosine, sine_table):
    half_width = values_in.shape[-1] // 2
    first_half = values_in[..., :half_width]
    second_half = values_in[..., half_width:]
    return jnp.concatenate(
        [
            first_half * cosine - second_half * sine_table,
            second_half * cosine + first_half * sine_table,
        ],
        axis=-1,
    )


def unrotate(grad_in, cosine, sine_table):
    half_width = grad_in.shape[-1] // 2
    first_half = grad_in[..., :half_width]
    second_half = grad_in[..., half_width:]
    return jnp.concatenate(
        [
            first_half * cosine + second_half * sine_table,
            second_half * cosine - first_half * sine_table,
        ],
        axis=-1,
    )


def norm_back(upstream, source, inv_scale, gain_vec):
    scaled = upstream * gain_vec
    gain_grad = jnp.sum(upstream * source * inv_scale, axis=0)
    grad_out = inv_scale * (
        scaled - source * inv_scale * inv_scale * jnp.mean(scaled * source, axis=-1, keepdims=True)
    )
    return (grad_out, gain_grad)


def on_device(
    tokens,
    lengths,
    routes,
    cotangent,
    first_gain,
    query_weight,
    key_matrix,
    value_matrix,
    output_weight,
    second_gain,
    router_weight,
    gate_up_weight,
    down_weight,
):
    seq_len, model_width = tokens.shape
    route_width = routes.shape[1]
    q_heads = query_weight.shape[1] // HEAD_DIM
    kv_heads = key_matrix.shape[1] // HEAD_DIM
    group_size = q_heads // kv_heads
    experts_all = router_weight.shape[1]
    local_experts = gate_up_weight.shape[1]
    inner_width = down_weight.shape[2]
    owners = lax.axis_size("expert")
    slot_count = 8 * max(
        seq_len // 32, (seq_len * route_width + 8 * experts_all - 1) // (8 * experts_all)
    )
    score_factor = HEAD_DIM ** (-0.5)
    gain_one, query_full, key_complete, value_complete, output_full, gain_two, router_full = (
        lax.all_gather(first_gain, "shard", axis=0, tiled=True),
        lax.all_gather(query_weight, "shard", axis=0, tiled=True),
        lax.all_gather(key_matrix, "shard", axis=0, tiled=True),
        lax.all_gather(value_matrix, "shard", axis=0, tiled=True),
        lax.all_gather(output_weight, "shard", axis=0, tiled=True),
        lax.all_gather(second_gain, "shard", axis=0, tiled=True),
        lax.all_gather(router_weight, "shard", axis=0, tiled=True),
    )
    gate_up_full, down_full = (
        lax.all_gather(gate_up_weight, "shard", axis=0, tiled=True),
        lax.all_gather(down_weight, "shard", axis=0, tiled=True),
    )
    gain_one = gain_one.astype(jnp.float32)
    gain_two = gain_two.astype(jnp.float32)
    cosine, sine_table = rope_tables(seq_len, HEAD_DIM)
    source = tokens.astype(jnp.float32)
    first_scale = lax.rsqrt(jnp.mean(source * source, axis=-1, keepdims=True) + norm_eps)
    first_norm_output = (source * first_scale * gain_one).astype(jnp.bfloat16)
    queries = rotate(
        product("za,ao->zo", first_norm_output, query_full).reshape(seq_len, q_heads, HEAD_DIM),
        cosine,
        sine_table,
    )
    queries = queries.astype(jnp.bfloat16).reshape(seq_len, kv_heads, group_size, HEAD_DIM)
    key_row_block = rotate(
        product("za,ao->zo", first_norm_output, key_complete).reshape(seq_len, kv_heads, HEAD_DIM),
        cosine,
        sine_table,
    ).astype(jnp.bfloat16)
    value_row_block = (
        product("za,ao->zo", first_norm_output, value_complete)
        .astype(jnp.bfloat16)
        .reshape(seq_len, kv_heads, HEAD_DIM)
    )
    position = jnp.arange(seq_len, dtype=jnp.int32)
    length = lengths[0]
    allowed = (position[None, :] <= position[:, None]) & (position[None, :] < length)
    scores = jnp.where(
        allowed, product("qhgd,khd->hgqk", queries, key_row_block) * score_factor, -1e30
    )
    row_max = jnp.max(scores, axis=-1, keepdims=True)
    shifted = jnp.exp(scores - row_max)
    row_total = jnp.sum(shifted, axis=-1, keepdims=True)
    log_total = row_max + jnp.log(row_total)
    probs_low = (shifted / row_total).astype(jnp.bfloat16)
    mixed_heads = (
        product("hgqk,khd->qhgd", probs_low, value_row_block)
        .reshape(seq_len, q_heads * HEAD_DIM)
        .astype(jnp.bfloat16)
    )
    hidden = source + product("sf,df->sd", mixed_heads, output_full)
    second_scale = lax.rsqrt(jnp.mean(hidden * hidden, axis=-1, keepdims=True) + norm_eps)
    second_normed = (hidden * second_scale * gain_two).astype(jnp.bfloat16)
    logits = product("sd,de->se", second_normed, router_full)
    chosen = (routes[:, :, None] == jnp.arange(experts_all, dtype=jnp.int32)).astype(jnp.float32)
    picked = jnp.sum(chosen * logits[:, None, :], axis=-1)
    gate_soft = jax.nn.softmax(picked, axis=-1)
    valid_rows = (position < length).astype(jnp.float32)
    routed = jnp.sum(chosen, axis=1) * valid_rows[:, None]
    earlier = (position[None, :] < position[:, None]).astype(jnp.bfloat16)
    rank_rows = product("st,te->se", earlier, routed.astype(jnp.bfloat16))
    slot_ids = jnp.arange(slot_count, dtype=jnp.float32)
    placing = (routed.T[:, None, :] * (rank_rows.T[:, None, :] == slot_ids[None, :, None])).astype(
        jnp.bfloat16
    )
    outgoing = (
        product("ems,sd->emd", placing, second_normed)
        .astype(jnp.bfloat16)
        .reshape(owners, local_experts, slot_count, model_width)
    )
    row_block = lax.all_to_all(outgoing, "expert", split_axis=0, concat_axis=0, tiled=True)
    both_pre = product("oemd,def->oemf", row_block, gate_up_full)
    active = (jax.nn.silu(both_pre[..., :inner_width]) * both_pre[..., inner_width:]).astype(
        jnp.bfloat16
    )
    answer = product("oemf,def->oemd", active, down_full).astype(jnp.bfloat16)
    returned = lax.all_to_all(answer, "expert", split_axis=0, concat_axis=0, tiled=True).reshape(
        experts_all, slot_count, model_width
    )
    gate_full = product("ske,sk->se", chosen.astype(jnp.bfloat16), gate_soft.astype(jnp.bfloat16))
    placing_float = placing.astype(jnp.float32)
    combine = (placing_float * gate_full.T[:, None, :]).astype(jnp.bfloat16)
    output = (hidden + product("ems,emd->sd", combine, returned)).astype(jnp.bfloat16)
    dout_full = cotangent.astype(jnp.float32) * valid_rows[:, None]
    dout_low = dout_full.astype(jnp.bfloat16)
    grad_rows = (
        product("ems,sd->emd", combine, dout_low)
        .astype(jnp.bfloat16)
        .reshape(owners, local_experts, slot_count, model_width)
    )
    incoming = lax.all_to_all(grad_rows, "expert", split_axis=0, concat_axis=0, tiled=True)
    answer_dot = product("emd,sd->ems", returned, dout_low)
    gate_grad_full = jnp.sum(placing_float * answer_dot, axis=1)
    gate_grad = jnp.sum(chosen * gate_grad_full.T[:, None, :], axis=-1)
    inner_sum = jnp.sum(gate_soft * gate_grad, axis=-1, keepdims=True)
    picked_grad = gate_soft * (gate_grad - inner_sum)
    logits_grad = jnp.sum(chosen * picked_grad[:, :, None], axis=1).astype(jnp.bfloat16)
    router_term = product("sd,se->de", second_normed, logits_grad)
    gate_up_full, down_full = (
        lax.all_gather(gate_up_weight, "shard", axis=0, tiled=True),
        lax.all_gather(down_weight, "shard", axis=0, tiled=True),
    )
    gate_part = both_pre[..., :inner_width]
    up_part = both_pre[..., inner_width:]
    sigmoid_gate = jax.nn.sigmoid(gate_part)
    silu_gate = gate_part * sigmoid_gate
    active_again = (silu_gate * up_part).astype(jnp.bfloat16)
    active_grad = product("oemd,def->oemf", incoming, down_full)
    both_grad = jnp.concatenate(
        [
            active_grad * up_part * sigmoid_gate * (1.0 + gate_part * (1.0 - sigmoid_gate)),
            active_grad * silu_gate,
        ],
        axis=-1,
    ).astype(jnp.bfloat16)
    row_grad = product("oemf,def->oemd", both_grad, gate_up_full).astype(jnp.bfloat16)
    gate_up_term = product("oemd,oemf->def", row_block, both_grad)
    down_term = product("oemd,oemf->def", incoming, active_again)
    back_rows = lax.all_to_all(row_grad, "expert", split_axis=0, concat_axis=0, tiled=True).reshape(
        experts_all, slot_count, model_width
    )
    gate_up_total, down_total = (
        lax.psum_scatter(
            gate_up_term.astype(jnp.bfloat16), "shard", scatter_dimension=0, tiled=True
        ).astype(jnp.float32),
        lax.psum_scatter(
            down_term.astype(jnp.bfloat16), "shard", scatter_dimension=0, tiled=True
        ).astype(jnp.float32),
    )
    normed_grad = product("ems,emd->sd", placing, back_rows) + product(
        "se,de->sd", logits_grad, router_full
    )
    hidden_grad, second_gain_term = norm_back(normed_grad, hidden, second_scale, gain_two)
    hidden_grad = hidden_grad + dout_full
    attn_grad = hidden_grad.astype(jnp.bfloat16)
    output_term = product("sd,sf->df", attn_grad, mixed_heads)
    mixed_grad = (
        product("za,ao->zo", attn_grad, output_full)
        .astype(jnp.bfloat16)
        .reshape(seq_len, kv_heads, group_size, HEAD_DIM)
    )
    scores_again = jnp.where(
        allowed, product("qhgd,khd->hgqk", queries, key_row_block) * score_factor, -1e30
    )
    probs_again = jnp.exp(scores_again - log_total)
    probs_grad = product("qhgd,khd->hgqk", mixed_grad, value_row_block)
    row_inner = jnp.sum(probs_again * probs_grad, axis=-1, keepdims=True)
    scores_grad = (probs_again * (probs_grad - row_inner)).astype(jnp.bfloat16)
    query_back = product("hgqk,khd->qhgd", scores_grad, key_row_block) * score_factor
    key_back = product("hgqk,qhgd->khd", scores_grad, queries) * score_factor
    value_back = product("hgqk,qhgd->khd", probs_again.astype(jnp.bfloat16), mixed_grad)
    query_pre = (
        unrotate(query_back.reshape(seq_len, q_heads, HEAD_DIM), cosine, sine_table)
        .astype(jnp.bfloat16)
        .reshape(seq_len, q_heads * HEAD_DIM)
    )
    key_pre = (
        unrotate(key_back, cosine, sine_table)
        .astype(jnp.bfloat16)
        .reshape(seq_len, kv_heads * HEAD_DIM)
    )
    value_pre = value_back.astype(jnp.bfloat16).reshape(seq_len, kv_heads * HEAD_DIM)
    query_term = product("sd,sf->df", first_norm_output, query_pre)
    key_term = product("sd,sf->df", first_norm_output, key_pre)
    value_term = product("sd,sf->df", first_norm_output, value_pre)
    normed1_grad = (
        product("sf,df->sd", query_pre, query_full)
        + product("sf,df->sd", key_pre, key_complete)
        + product("sf,df->sd", value_pre, value_complete)
    )
    tokens_grad, first_gain_term = norm_back(normed1_grad, source, first_scale, gain_one)
    tokens_grad = tokens_grad + hidden_grad
    mixer_sums = (
        lax.psum_scatter(
            first_gain_term.astype(jnp.bfloat16), "shard", scatter_dimension=0, tiled=True
        ).astype(jnp.float32),
        lax.psum_scatter(
            query_term.astype(jnp.bfloat16), "shard", scatter_dimension=0, tiled=True
        ).astype(jnp.float32),
        lax.psum_scatter(
            key_term.astype(jnp.bfloat16), "shard", scatter_dimension=0, tiled=True
        ).astype(jnp.float32),
        lax.psum_scatter(
            value_term.astype(jnp.bfloat16), "shard", scatter_dimension=0, tiled=True
        ).astype(jnp.float32),
        lax.psum_scatter(
            output_term.astype(jnp.bfloat16), "shard", scatter_dimension=0, tiled=True
        ).astype(jnp.float32),
        lax.psum_scatter(
            second_gain_term.astype(jnp.bfloat16), "shard", scatter_dimension=0, tiled=True
        ).astype(jnp.float32),
        lax.psum_scatter(
            router_term.astype(jnp.bfloat16), "shard", scatter_dimension=0, tiled=True
        ).astype(jnp.float32),
    )
    mixer_sums = (
        lax.psum(mixer_sums[0].astype(jnp.bfloat16), "expert").astype(jnp.float32),
        lax.psum(mixer_sums[1].astype(jnp.bfloat16), "expert").astype(jnp.float32),
        lax.psum(mixer_sums[2].astype(jnp.bfloat16), "expert").astype(jnp.float32),
        lax.psum(mixer_sums[3].astype(jnp.bfloat16), "expert").astype(jnp.float32),
        lax.psum(mixer_sums[4].astype(jnp.bfloat16), "expert").astype(jnp.float32),
        lax.psum(mixer_sums[5].astype(jnp.bfloat16), "expert").astype(jnp.float32),
        lax.psum(mixer_sums[6].astype(jnp.bfloat16), "expert").astype(jnp.float32),
    )
    return (
        output,
        tokens_grad,
        mixer_sums[0],
        mixer_sums[1],
        mixer_sums[2],
        mixer_sums[3],
        mixer_sums[4],
        mixer_sums[5],
        mixer_sums[6],
        gate_up_total,
        down_total,
    )


def solution(mesh):
    placed = (
        P(("expert", "shard"), None),
        P(("expert", "shard")),
        P(("expert", "shard"), None),
        P(("expert", "shard"), None),
        P("shard"),
        P("shard", None),
        P("shard", None),
        P("shard", None),
        P("shard", None),
        P("shard"),
        P("shard", None),
        P("shard", "expert", None),
        P("shard", "expert", None),
    )
    return jax.shard_map(
        on_device,
        mesh=mesh,
        in_specs=placed,
        out_specs=(
            P(("expert", "shard"), None),
            P(("expert", "shard"), None),
            P("shard"),
            P("shard", None),
            P("shard", None),
            P("shard", None),
            P("shard", None),
            P("shard"),
            P("shard", None),
            P("shard", "expert", None),
            P("shard", "expert", None),
        ),
        check_vma=False,
    )
```

profile of v0, /device:TPU:0, one launch (start us, length us, event | category | flops | bytes accessed | tf_op | source)
XLA Modules:
  0.0 1752.7 jit_solution(12676118598216443781)
XLA Ops:
  13.8 23.5 %all-reduce.5 = (bf16[1536]{0:T(1024)(128)(2,1)S(1)}, bf16[1536]{0:T(1024)(128)(2,1)S(1)}) all-reduce(bf16[1536]{0:T(1024)(128)(2,1)S(1)} %dynamic-update-slice, bf16[1536]{0:T(1024)(128)(2,1)S(1)} %dynamic-update-slice.1), channel_id=1, replica_groups=mesh['expert'=4,'shard'=8] {'shard'}, use_global_device_ids=true, to_apply=%add | all-reduce | flops 3072 | bytes 12288
  38.1 19.4 %all-gather.8.cloned.1.call-done = bf16[1536,512]{1,0:T(8,128)(2,1)} async-done(((bf16[192,512]{1,0:T(8,128)(2,1)}), bf16[1536,512]{1,0:T(8,128)(2,1)}) %all-gather.8.cloned.1.call-update) | async-done | bytes 1572880 | tf_op jit(solution)/shard_map/all_gather | solution.py:88
  59.7 42.6 %all-gather.10.cloned.1.call-done = bf16[1536,512]{1,0:T(8,128)(2,1)} async-done(((bf16[192,512]{1,0:T(8,128)(2,1)}), bf16[1536,512]{1,0:T(8,128)(2,1)}) %all-gather.10.cloned.1.call-update) | async-done | bytes 1572880 | tf_op jit(solution)/shard_map/all_gather | solution.py:87
  104.6 77.6 %all-gather.12.cloned.1.call-done = bf16[1536,1536]{1,0:T(8,128)(2,1)} async-done(((bf16[192,1536]{1,0:T(8,128)(2,1)}), bf16[1536,1536]{1,0:T(8,128)(2,1)}) %all-gather.12.cloned.1.call-update) | async-done | bytes 4718608 | tf_op jit(solution)/shard_map/all_gather | solution.py:86
  191.8 70.1 %all-gather.14.cloned.1.call-done = bf16[1536,1536]{1,0:T(8,128)(2,1)} async-done(((bf16[192,1536]{1,0:T(8,128)(2,1)}), bf16[1536,1536]{1,0:T(8,128)(2,1)}) %all-gather.14.cloned.1.call-update) | async-done | bytes 4718608 | tf_op jit(solution)/shard_map/all_gather | solution.py:89
  267.9 75.5 %all_to_all.20 = bf16[4,5,104,1536]{3,2,1,0:T(8,128)(2,1)} all-to-all(bf16[4,5,104,1536]{3,2,1,0:T(8,128)(2,1)S(1)} %bitcast.174), channel_id=1, replica_groups=mesh['expert'=4,'shard'=8] {'expert'}, dimensions={0} | all-to-all | bytes 12779520 | tf_op jit(solution)/shard_map/all_to_all | solution.py:155
  343.4 133.5 %all-gather.16.cloned.1.call-done = bf16[1536,5,1024]{2,0,1:T(8,128)(2,1)} async-done(((bf16[192,5,1024]{2,0,1:T(8,128)(2,1)}), bf16[1536,5,1024]{2,0,1:T(8,128)(2,1)}) %all-gather.16.cloned.1.call-update) | async-done | bytes 15728656 | tf_op jit(solution)/shard_map/all_gather | solution.py:94
  476.9 12.1 fusion.26
  495.2 99.9 %all-gather.18.cloned.1.call-done = bf16[1536,5,512]{2,0,1:T(8,128)(2,1)} async-done(((bf16[192,5,512]{2,0,1:T(8,128)(2,1)}), bf16[1536,5,512]{2,0,1:T(8,128)(2,1)}) %all-gather.18.cloned.1.call-update) | async-done | bytes 7864336 | tf_op jit(solution)/shard_map/all_gather | solution.py:95
  616.5 30.6 %all-gather = bf16[8,192,20]{1,2,0:T(8,128)(2,1)S(1)} all-gather(bf16[1,192,20]{1,2,0:T(8,128)(2,1)S(1)} %bitcast.202), channel_id=1, replica_groups=mesh['expert'=4,'shard'=8] {'shard'}, dimensions={0}, use_global_device_ids=true | all-gather | bytes 69120 | tf_op jit(solution)/shard_map/all_gather | solution.py:91
  647.5 40.7 %all-to-all-done.1 = bf16[4,5,104,1536]{3,2,1,0:T(8,128)(2,1)} async-done(((bf16[4,5,104,1536]{3,2,1,0:T(8,128)(2,1)}), bf16[4,5,104,1536]{3,2,1,0:T(8,128)(2,1)}, u32[]{:S(2)}, u32[]{:S(2)}) %all-to-all-start.1) | async-done | bytes 6389792 | tf_op jit(solution)/shard_map/all_to_all | solution.py:161
  696.6 75.7 %all_to_all.21 = bf16[4,5,104,1536]{3,2,1,0:T(8,128)(2,1)} all-to-all(bf16[4,5,104,1536]{3,2,1,0:T(8,128)(2,1)S(1)} %bitcast.180), channel_id=1, replica_groups=mesh['expert'=4,'shard'=8] {'expert'}, dimensions={0} | all-to-all | bytes 12779520 | tf_op jit(solution)/shard_map/all_to_all | solution.py:175
  772.3 14.0 fusion.23
  786.2 13.4 convert_bitcast_fusion
  811.1 71.5 %all-to-all-done.3 = bf16[4,5,104,1536]{3,2,1,0:T(8,128)(2,1)} async-done(((bf16[4,5,104,1536]{3,2,1,0:T(8,128)(2,1)}), bf16[4,5,104,1536]{3,2,1,0:T(8,128)(2,1)}, u32[]{:S(2)}, u32[]{:S(2)}) %all-to-all-start.3) | async-done | bytes 6389792 | tf_op jit(solution)/shard_map/all_to_all | solution.py:203
  931.9 34.8 %reduce-scatter.18.cloned.1.call-done = bf16[192,512]{1,0:T(8,128)(2,1)} async-done(((bf16[1536,512]{1,0:T(8,128)(2,1)}), bf16[192,512]{1,0:T(8,128)(2,1)}) %reduce-scatter.18.cloned.1.call-update) | async-done | bytes 196624 | tf_op jit(solution)/shard_map/reduce_scatter | solution.py:267
  966.7 68.2 %reduce-scatter.16.cloned.1.call-done = bf16[192,512]{1,0:T(8,128)(2,1)} async-done(((bf16[1536,512]{1,0:T(8,128)(2,1)}), bf16[192,512]{1,0:T(8,128)(2,1)}) %reduce-scatter.16.cloned.1.call-update) | async-done | bytes 196624 | tf_op jit(solution)/shard_map/reduce_scatter | solution.py:264
  1034.9 98.3 %reduce-scatter.20.cloned.1.call-done = bf16[192,1536]{1,0:T(8,128)(2,1)} async-done(((bf16[1536,1536]{1,0:T(8,128)(2,1)}), bf16[192,1536]{1,0:T(8,128)(2,1)}) %reduce-scatter.20.cloned.1.call-update) | async-done | bytes 589840 | tf_op jit(solution)/shard_map/reduce_scatter | solution.py:270
  1133.2 98.8 %reduce-scatter.14.cloned.1.call-done = bf16[192,1536]{1,0:T(8,128)(2,1)} async-done(((bf16[1536,1536]{1,0:T(8,128)(2,1)}), bf16[192,1536]{1,0:T(8,128)(2,1)}) %reduce-scatter.14.cloned.1.call-update) | async-done | bytes 589840 | tf_op jit(solution)/shard_map/reduce_scatter | solution.py:261
  1253.9 15.1 bitcast_convert_fusion
  1269.0 20.8 %copy.124 = bf16[1536,5120]{1,0:T(8,128)(2,1)} copy(bf16[1536,5120]{0,1:T(8,128)(2,1)} %bitcast.175) | data formatting | bytes 31457280
  1306.1 19.7 %all-reduce.4 = (bf16[1536]{0:T(1024)(128)(2,1)S(1)}, bf16[1536]{0:T(1024)(128)(2,1)S(1)}) all-reduce(bf16[1536]{0:T(1024)(128)(2,1)S(1)} %get-tuple-element.57, bf16[1536]{0:T(1024)(128)(2,1)S(1)} %copy-done.32), channel_id=2, replica_groups=mesh['expert'=4,'shard'=8] {'shard'}, use_global_device_ids=true, to_apply=%region_16.17.clone | all-reduce | flops 3072 | bytes 12288
  1349.3 136.9 %reduce-scatter.26.cloned.1.call-done = bf16[192,2560]{1,0:T(8,128)(2,1)} async-done(((bf16[1536,2560]{1,0:T(8,128)(2,1)}), bf16[192,2560]{1,0:T(8,128)(2,1)}) %reduce-scatter.26.cloned.1.call-update) | async-done | bytes 983056
  1489.4 250.7 %reduce-scatter.24.cloned.1.call-done = bf16[192,5120]{1,0:T(8,128)(2,1)} async-done(((bf16[1536,5120]{1,0:T(8,128)(2,1)}), bf16[192,5120]{1,0:T(8,128)(2,1)}) %reduce-scatter.24.cloned.1.call-update) | async-done | bytes 1966096
  (204 shorter events, 192.2 us)
Async XLA Ops:
  7.2 50.3 %all-gather.8.cloned.1.call-start = ((), (), s32[]{:S(2)}) async-start(), calls=%async_computation.11 | async-start | bytes 1769472 | tf_op jit(solution)/shard_map/all_gather | solution.py:88
  7.9 94.4 %all-gather.10.cloned.1.call-start = ((), (), s32[]{:S(2)}) async-start(), calls=%async_computation.12 | async-start | bytes 1769472 | tf_op jit(solution)/shard_map/all_gather | solution.py:87
  8.7 173.5 %all-gather.12.cloned.1.call-start = ((), (), s32[]{:S(2)}) async-start(), calls=%async_computation.13 | async-start | bytes 5308416 | tf_op jit(solution)/shard_map/all_gather | solution.py:86
  9.4 252.5 %all-gather.14.cloned.1.call-start = ((), (), s32[]{:S(2)}) async-start(), calls=%async_computation.14 | async-start | bytes 5308416 | tf_op jit(solution)/shard_map/all_gather | solution.py:89
  10.0 466.8 %all-gather.16.cloned.1.call-start = ((), (), s32[]{:S(2)}) async-start(), calls=%async_computation.15 | async-start | bytes 17694720 | tf_op jit(solution)/shard_map/all_gather | solution.py:94
  10.6 584.4 %all-gather.18.cloned.1.call-start = ((), (), s32[]{:S(2)}) async-start(), calls=%async_computation.16 | async-start | bytes 8847360 | tf_op jit(solution)/shard_map/all_gather | solution.py:95
  11.9 676.4 %copy-start.36 = (f32[256]{0:T(256)}, f32[256]{0:T(256)S(1)}, u32[]{:S(2)}) copy-start(f32[256]{0:T(256)S(1)} %fusion.100) | copy-start | bytes 3076
  37.6 887.8 %copy-start.24 = (f32[256]{0:T(256)}, f32[256]{0:T(256)S(1)}, u32[]{:S(2)}) copy-start(f32[256]{0:T(256)S(1)} %add_rsqrt_fusion.1) | copy-start | bytes 3076
  37.6 845.0 %copy-start.26 = (bf16[20,256]{1,0:T(8,128)(2,1)}, bf16[20,256]{1,0:T(8,128)(2,1)S(1)}, u32[]{:S(2)}) copy-start(bf16[20,256]{1,0:T(8,128)(2,1)S(1)} %multiply_bitcast_fusion) | copy-start | bytes 30724
  37.8 844.8 %copy-start.28 = (f32[20,256]{1,0:T(8,128)}, f32[20,256]{1,0:T(8,128)S(1)}, u32[]{:S(2)}) copy-start(f32[20,256]{1,0:T(8,128)S(1)} %fusion.83) | copy-start | bytes 61444
  59.7 129.4 %copy-start.15 = (bf16[256,512]{0,1:T(8,128)(2,1)}, bf16[256,512]{0,1:T(8,128)(2,1)S(1)}, u32[]{:S(2)}) copy-start(bf16[256,512]{0,1:T(8,128)(2,1)S(1)} %copy.83) | copy-start | bytes 786436
  104.6 82.2 %copy-start.19 = (bf16[256,8,32]{0,2,1:T(8,128)(2,1)}, bf16[256,8,32]{0,2,1:T(8,128)(2,1)S(1)}, u32[]{:S(2)}) copy-start(bf16[256,8,32]{0,2,1:T(8,128)(2,1)S(1)} %get-tuple-element.82) | copy-start | bytes 393220
  265.8 621.6 %copy-start.3 = (f32[256,1536]{1,0:T(8,128)}, f32[256,1536]{1,0:T(8,128)S(1)}, u32[]{:S(2)}) copy-start(f32[256,1536]{1,0:T(8,128)S(1)} %get-tuple-element.93) | copy-start | bytes 4718596
  611.1 77.1 %all-to-all-start.1 = ((bf16[4,5,104,1536]{3,2,1,0:T(8,128)(2,1)}), bf16[4,5,104,1536]{3,2,1,0:T(8,128)(2,1)}, u32[]{:S(2)}, u32[]{:S(2)}) async-start(bf16[4,5,104,1536]{3,2,1,0:T(8,128)(2,1)} %copy.89), calls=%async_computation.1 | async-start | bytes 12779520 | tf_op jit(solution)/shard_map/all_to_all | solution.py:161
  693.5 194.0 %copy-start.21 = (bf16[256,20]{0,1:T(8,128)(2,1)}, bf16[256,20]{0,1:T(8,128)(2,1)S(1)}, u32[]{:S(2)}) copy-start(bf16[256,20]{0,1:T(8,128)(2,1)S(1)} %get-tuple-element.59) | copy-start | bytes 30724
  805.6 77.0 %all-to-all-start.3 = ((bf16[4,5,104,1536]{3,2,1,0:T(8,128)(2,1)}), bf16[4,5,104,1536]{3,2,1,0:T(8,128)(2,1)}, u32[]{:S(2)}, u32[]{:S(2)}) async-start(bf16[4,5,104,1536]{3,2,1,0:T(8,128)(2,1)} %copy.91), calls=%async_computation.3 | async-start | bytes 12779520 | tf_op jit(solution)/shard_map/all_to_all | solution.py:203
  810.9 155.8 %reduce-scatter.18.cloned.1.call-start = ((), (), s32[]{:S(2)}) async-start(), calls=%async_computation.19 | async-start | bytes 1769472 | tf_op jit(solution)/shard_map/reduce_scatter | solution.py:267
  903.7 131.2 %reduce-scatter.16.cloned.1.call-start = ((), (), s32[]{:S(2)}) async-start(), calls=%async_computation.18 | async-start | bytes 1769472 | tf_op jit(solution)/shard_map/reduce_scatter | solution.py:264
  917.2 216.0 %reduce-scatter.20.cloned.1.call-start = ((), (), s32[]{:S(2)}) async-start(), calls=%async_computation.20 | async-start | bytes 5308416 | tf_op jit(solution)/shard_map/reduce_scatter | solution.py:270
  922.0 310.1 %reduce-scatter.14.cloned.1.call-start = ((), (), s32[]{:S(2)}) async-start(), calls=%async_computation.17 | async-start | bytes 5308416 | tf_op jit(solution)/shard_map/reduce_scatter | solution.py:261
  929.9 367.9 %reduce-scatter.22.cloned.1.call-start = ((), (), s32[]{:S(2)}) async-start(), calls=%async_computation.21 | async-start | bytes 442368
  931.8 410.6 %all-reduce.10.cloned.1.call-start = ((), (), s32[]{:S(2)}) async-start(), calls=%async_computation.24 | async-start | bytes 3145728 | tf_op jit(solution)/shard_map/psum | solution.py:282
  1232.1 254.1 %reduce-scatter.26.cloned.1.call-start = ((), (), s32[]{:S(2)}) async-start(), calls=%async_computation.23 | async-start | bytes 8847360
  1253.6 486.4 %reduce-scatter.24.cloned.1.call-start = ((), (), s32[]{:S(2)}) async-start(), calls=%async_computation.22 | async-start | bytes 17694720
  (33 other events, 294.0 us)
Sparse Core Ops, SparseCore 0:
  10.2 47.3 all-gather.7
  59.7 42.5 all-gather.9
  104.5 77.6 all-gather.11
  184.2 77.6 all-gather.13
  264.0 212.8 all-gather.15
  478.9 116.1 all-gather.17
  903.8 62.8 reduce-scatter.17
  970.7 64.1 reduce-scatter.15
  1038.6 94.6 reduce-scatter.19
  1136.7 95.3 reduce-scatter.13
  1235.9 61.8 reduce-scatter.21
  1300.2 42.1 all-reduce.9
  1346.1 140.1 reduce-scatter.25
  1489.7 250.3 reduce-scatter.23
where the time goes:
time: 1760 us; the launch traced here: 1750 us
  waiting for transfers between devices  1250 us (71%)
  blocking collectives  237 us (13%)
  matrix products  149 us (8%)
  local copies, waits for them, and re-layouts  66.5 us (4%)
  other arithmetic  23.9 us (1%)
    unnamed x17, waiting for transfers between devices  392 us
    dot_general x33, matrix products, product(): return jnp.einsum(form, left, right, preferred_element_type=jnp.float32)  149 us
    all_gather x1, waiting for transfers between devices, on_device(): lax.all_gather(gate_up_weight, 'shard', axis=0, tiled=True)  133 us
    all_gather x1, waiting for transfers between devices, on_device(): lax.all_gather(down_weight, 'shard', axis=0, tiled=True)  99.9 us
    reduce_scatter x1, waiting for transfers between devices, on_device(): lax.psum_scatter(query_term.astype(jnp.bfloat16), 'shard', scatter_dimens...  98.8 us
    reduce_scatter x1, waiting for transfers between devices, on_device(): lax.psum_scatter(output_term.astype(jnp.bfloat16), 'shard', scatter_dimen...  98.3 us
    all_gather x1, waiting for transfers between devices, on_device(): lax.all_gather(query_weight, 'shard', axis=0, tiled=True)  77.6 us
    all_to_all x1, blocking collectives, on_device(): lax.all_to_all(grad_rows, 'expert', split_axis=0, concat_axis=0, tiled=True)  75.7 us
  transfers between devices with their start and end apart: 16, of which 15 were waited for; matrix products, arithmetic and copies ran while one was open for 8% of the time, Pallas kernels for 0%

commit v1 on v0

--- a/solution.py
+++ b/solution.py
@@ -5,6 +5,18 @@
 
 HEAD_DIM = 64
 norm_eps = 1e-06
+
+
+def doubled_up(shard, axis, dim):
+    ways, here, turn = (lax.axis_size(axis), lax.axis_index(axis), shard.shape[dim])
+    line, have = (shard, 1)
+    while have < ways:
+        line = jnp.concatenate(
+            [line, lax.ppermute(line, axis, [(d, (d - have) % ways) for d in range(ways)])],
+            axis=dim,
+        )
+        have = 2 * have
+    return jnp.roll(line, here * turn, axis=dim)
 
 
 def product(form, left, right):
@@ -92,7 +104,7 @@
     )
     gate_up_full, down_full = (
         lax.all_gather(gate_up_weight, "shard", axis=0, tiled=True),
-        lax.all_gather(down_weight, "shard", axis=0, tiled=True),
+        doubled_up(down_weight, "shard", 0),
     )
     gain_one = gain_one.astype(jnp.float32)
     gain_two = gain_two.astype(jnp.float32)

time: 1760 us -> 1880 us (1.068)
  waiting for transfers between devices: 1250 us -> 1450 us
  blocking collectives: 237 us -> 105 us
    ppermute x0 -> x3, waiting for transfers between devices: none -> 333 us  [doubled_up(): lax.ppermute(line, axis, [(d, (d - have) % ways) for d in range(ways)])]
    all_to_all x2 -> x0, blocking collectives: 151 us -> none  [the longest x1 75.7 us: on_device(): lax.all_to_all(grad_rows, 'expert', split_axis=0, concat_axis=0, tiled=True)]
    all_gather x1, waiting for transfers between devices: 133 us -> 0.49 us  [on_device(): lax.all_gather(gate_up_weight, 'shard', axis=0, tiled=True)]
    all_gather x1, waiting for transfers between devices: 99.9 us -> 0.02 us  [on_device(): lax.all_gather(down_weight, 'shard', axis=0, tiled=True)]
    all_to_all x0 -> x2, waiting for transfers between devices: none -> 71.7 us  [the longest x1 71.7 us: on_device(): lax.all_to_all(grad_rows, 'expert', split_axis=0, concat_axis=0, tiled=True)]
    all_gather x1, waiting for transfers between devices: 42.6 us -> 80.9 us  [on_device(): lax.all_gather(key_matrix, 'shard', axis=0, tiled=True)]
    unnamed x98 -> x155, local copies, waits for them, and re-layouts: 52 us -> 66.1 us
  transfers between devices with their start and end apart: 16 -> 21, of which waited for: 15 -> 16; matrix products, arithmetic and copies ran while one was open for 8% -> 11% of each run, Pallas kernels for 0% -> 0%
where the time goes in v1:
time: 1880 us; the launch traced here: 1870 us
  waiting for transfers between devices  1450 us (77%)
  matrix products  154 us (8%)
  blocking collectives  105 us (6%)
  local copies, waits for them, and re-layouts  85 us (5%)
  starting transfers between devices  30.5 us (2%)
  other arithmetic  26.1 us (1%)
    unnamed x17, waiting for transfers between devices  395 us
    ppermute x3, waiting for transfers between devices, doubled_up(): lax.ppermute(line, axis, [(d, (d - have) % ways) for d in range(ways)])  333 us
    dot_general x33, matrix products, product(): return jnp.einsum(form, left, right, preferred_element_type=jnp.float32)  154 us
    reduce_scatter x1, waiting for transfers between devices, on_device(): lax.psum_scatter(output_term.astype(jnp.bfloat16), 'shard', scatter_dimen...  98.8 us
    reduce_scatter x1, waiting for transfers between devices, on_device(): lax.psum_scatter(query_term.astype(jnp.bfloat16), 'shard', scatter_dimens...  98.1 us
    all_gather x1, waiting for transfers between devices, on_device(): lax.all_gather(key_matrix, 'shard', axis=0, tiled=True)  80.9 us
    all_gather x1, waiting for transfers between devices, on_device(): lax.all_gather(query_weight, 'shard', axis=0, tiled=True)  77.6 us
    all_to_all x1, waiting for transfers between devices, on_device(): lax.all_to_all(grad_rows, 'expert', split_axis=0, concat_axis=0, tiled=True)  71.7 us
  transfers between devices with their start and end apart: 21, of which 16 were waited for; matrix products, arithmetic and copies ran while one was open for 11% of the time, Pallas kernels for 0%

profile of v1, /device:TPU:0, one launch (start us, length us, event | category | flops | bytes accessed | tf_op | source)
XLA Modules:
  0.0 1865.8 jit_solution(6028106457925464057)
XLA Ops:
  18.5 41.1 %all-reduce.5 = (bf16[1536]{0:T(1024)(128)(2,1)S(1)}, bf16[1536]{0:T(1024)(128)(2,1)S(1)}) all-reduce(bf16[1536]{0:T(1024)(128)(2,1)S(1)} %dynamic-update-slice, bf16[1536]{0:T(1024)(128)(2,1)S(1)} %dynamic-update-slice.1), channel_id=1, replica_groups=mesh['expert'=4,'shard'=8] {'shard'}, use_global_device_ids=true, to_apply=%add | all-reduce | flops 3072 | bytes 12288
  73.7 80.9 %all-gather.10.cloned.1.call-done = bf16[1536,512]{1,0:T(8,128)(2,1)} async-done(((bf16[192,512]{1,0:T(8,128)(2,1)}), bf16[1536,512]{1,0:T(8,128)(2,1)}) %all-gather.10.cloned.1.call-update) | async-done | bytes 1572880 | tf_op jit(solution)/shard_map/all_gather | solution.py:99
  156.9 77.6 %all-gather.12.cloned.1.call-done = bf16[1536,1536]{1,0:T(8,128)(2,1)} async-done(((bf16[192,1536]{1,0:T(8,128)(2,1)}), bf16[1536,1536]{1,0:T(8,128)(2,1)}) %all-gather.12.cloned.1.call-update) | async-done | bytes 4718608 | tf_op jit(solution)/shard_map/all_gather | solution.py:98
  244.2 70.0 %all-gather.14.cloned.1.call-done = bf16[1536,1536]{1,0:T(8,128)(2,1)} async-done(((bf16[192,1536]{1,0:T(8,128)(2,1)}), bf16[1536,1536]{1,0:T(8,128)(2,1)}) %all-gather.14.cloned.1.call-update) | async-done | bytes 4718608 | tf_op jit(solution)/shard_map/all_gather | solution.py:101
  340.6 332.8 %collective-permute-done.2 = bf16[768,5,512]{2,0,1:T(8,128)(2,1)} collective-permute-done((bf16[768,5,512]{2,0,1:T(8,128)(2,1)}, bf16[768,5,512]{2,0,1:T(8,128)(2,1)}, u32[]{:S(2)}, u32[]{:S(2)}) %collective-permute-start.2) | collective-permute-done | bytes 3932192 | tf_op jit(solution)/shard_map/ppermute | solution.py:15
  688.0 12.1 fusion.27
  727.8 32.1 %all-gather = bf16[8,192,20]{1,2,0:T(8,128)(2,1)S(1)} all-gather(bf16[1,192,20]{1,2,0:T(8,128)(2,1)S(1)} %bitcast.205), channel_id=1, replica_groups=mesh['expert'=4,'shard'=8] {'shard'}, dimensions={0}, use_global_device_ids=true | all-gather | bytes 69120 | tf_op jit(solution)/shard_map/all_gather | solution.py:103
  760.3 39.1 %all-to-all-done.1 = bf16[4,5,104,1536]{3,2,1,0:T(8,128)(2,1)} async-done(((bf16[4,5,104,1536]{3,2,1,0:T(8,128)(2,1)}), bf16[4,5,104,1536]{3,2,1,0:T(8,128)(2,1)}, u32[]{:S(2)}, u32[]{:S(2)}) %all-to-all-start.1) | async-done | bytes 6389792 | tf_op jit(solution)/shard_map/all_to_all | solution.py:173
  814.6 71.7 %all-to-all-done.2 = bf16[4,5,104,1536]{3,2,1,0:T(8,128)(2,1)} async-done(((bf16[4,5,104,1536]{3,2,1,0:T(8,128)(2,1)}), bf16[4,5,104,1536]{3,2,1,0:T(8,128)(2,1)}, u32[]{:S(2)}, u32[]{:S(2)}) %all-to-all-start.2) | async-done | bytes 6389792 | tf_op jit(solution)/shard_map/all_to_all | solution.py:187
  886.3 14.0 fusion.24
  900.3 13.3 convert_bitcast_fusion
  925.4 71.4 %all-to-all-done.3 = bf16[4,5,104,1536]{3,2,1,0:T(8,128)(2,1)} async-done(((bf16[4,5,104,1536]{3,2,1,0:T(8,128)(2,1)}), bf16[4,5,104,1536]{3,2,1,0:T(8,128)(2,1)}, u32[]{:S(2)}, u32[]{:S(2)}) %all-to-all-start.3) | async-done | bytes 6389792 | tf_op jit(solution)/shard_map/all_to_all | solution.py:215
  1044.1 35.8 %reduce-scatter.18.cloned.1.call-done = bf16[192,512]{1,0:T(8,128)(2,1)} async-done(((bf16[1536,512]{1,0:T(8,128)(2,1)}), bf16[192,512]{1,0:T(8,128)(2,1)}) %reduce-scatter.18.cloned.1.call-update) | async-done | bytes 196624 | tf_op jit(solution)/shard_map/reduce_scatter | solution.py:279
  1079.9 68.3 %reduce-scatter.16.cloned.1.call-done = bf16[192,512]{1,0:T(8,128)(2,1)} async-done(((bf16[1536,512]{1,0:T(8,128)(2,1)}), bf16[192,512]{1,0:T(8,128)(2,1)}) %reduce-scatter.16.cloned.1.call-update) | async-done | bytes 196624 | tf_op jit(solution)/shard_map/reduce_scatter | solution.py:276
  1148.3 98.1 %reduce-scatter.14.cloned.1.call-done = bf16[192,1536]{1,0:T(8,128)(2,1)} async-done(((bf16[1536,1536]{1,0:T(8,128)(2,1)}), bf16[192,1536]{1,0:T(8,128)(2,1)}) %reduce-scatter.14.cloned.1.call-update) | async-done | bytes 589840 | tf_op jit(solution)/shard_map/reduce_scatter | solution.py:273
  1246.4 98.8 %reduce-scatter.20.cloned.1.call-done = bf16[192,1536]{1,0:T(8,128)(2,1)} async-done(((bf16[1536,1536]{1,0:T(8,128)(2,1)}), bf16[192,1536]{1,0:T(8,128)(2,1)}) %reduce-scatter.20.cloned.1.call-update) | async-done | bytes 589840 | tf_op jit(solution)/shard_map/reduce_scatter | solution.py:282
  1345.3 10.8 bitcast_convert_fusion.1
  1356.1 10.4 copy.127
  1366.6 15.2 bitcast_convert_fusion
  1381.8 19.6 %copy.125 = bf16[1536,5120]{1,0:T(8,128)(2,1)} copy(bf16[1536,5120]{0,1:T(8,128)(2,1)} %bitcast.178) | data formatting | bytes 31457280
  1419.3 19.7 %all-reduce.4 = (bf16[1536]{0:T(1024)(128)(2,1)S(1)}, bf16[1536]{0:T(1024)(128)(2,1)S(1)}) all-reduce(bf16[1536]{0:T(1024)(128)(2,1)S(1)} %get-tuple-element.57, bf16[1536]{0:T(1024)(128)(2,1)S(1)} %copy-done.57), channel_id=2, replica_groups=mesh['expert'=4,'shard'=8] {'shard'}, use_global_device_ids=true, to_apply=%region_16.17.clone | all-reduce | flops 3072 | bytes 12288
  1439.2 11.7 all-reduce.6
  1460.7 138.7 %reduce-scatter.26.cloned.1.call-done = bf16[192,2560]{1,0:T(8,128)(2,1)} async-done(((bf16[1536,2560]{1,0:T(8,128)(2,1)}), bf16[192,2560]{1,0:T(8,128)(2,1)}) %reduce-scatter.26.cloned.1.call-update) | async-done | bytes 983056
  1602.5 250.7 %reduce-scatter.24.cloned.1.call-done = bf16[192,5120]{1,0:T(8,128)(2,1)} async-done(((bf16[1536,5120]{1,0:T(8,128)(2,1)}), bf16[192,5120]{1,0:T(8,128)(2,1)}) %reduce-scatter.24.cloned.1.call-update) | async-done | bytes 1966096
  (272 shorter events, 214.4 us)
Async XLA Ops:
  7.2 64.3 %all-gather.8.cloned.1.call-start = ((), (), s32[]{:S(2)}) async-start(), calls=%async_computation.11 | async-start | bytes 1769472 | tf_op jit(solution)/shard_map/all_gather | solution.py:100
  8.0 146.6 %all-gather.10.cloned.1.call-start = ((), (), s32[]{:S(2)}) async-start(), calls=%async_computation.12 | async-start | bytes 1769472 | tf_op jit(solution)/shard_map/all_gather | solution.py:99
  8.7 225.8 %all-gather.12.cloned.1.call-start = ((), (), s32[]{:S(2)}) async-start(), calls=%async_computation.13 | async-start | bytes 5308416 | tf_op jit(solution)/shard_map/all_gather | solution.py:98
  9.5 304.8 %all-gather.14.cloned.1.call-start = ((), (), s32[]{:S(2)}) async-start(), calls=%async_computation.14 | async-start | bytes 5308416 | tf_op jit(solution)/shard_map/all_gather | solution.py:101
  10.0 678.0 %all-gather.16.cloned.1.call-start = ((), (), s32[]{:S(2)}) async-start(), calls=%async_computation.15 | async-start | bytes 17694720 | tf_op jit(solution)/shard_map/all_gather | solution.py:106
  10.6 51.8 %collective-permute-start = (bf16[192,5,512]{2,0,1:T(8,128)(2,1)S(1)}, bf16[192,5,512]{2,0,1:T(8,128)(2,1)S(1)}, u32[]{:S(2)}, u32[]{:S(2)}) collective-permute-start(bf16[192,5,512]{2,0,1:T(8,128)(2,1)S(1)} %copy-done.3), channel_id=1, source_target_pairs={{0,7},{1,0},{2,1},{3,2},{4,3},{5,4},{6,5},{7,6},{8,15},{9,8},{10,9... | collective-permute-start | bytes 2949128 | tf_op jit(solution)/shard_map/ppermute | solution.py:15
  62.3 176.6 %copy-start.23 = (f32[256,32]{0,1:T(8,128)}, f32[256,32]{0,1:T(8,128)S(1)}, u32[]{:S(2)}) copy-start(f32[256,32]{0,1:T(8,128)S(1)} %get-tuple-element.88) | copy-start | bytes 98308
  62.3 176.6 %copy-start.26 = (f32[256,32]{0,1:T(8,128)}, f32[256,32]{0,1:T(8,128)S(1)}, u32[]{:S(2)}) copy-start(f32[256,32]{0,1:T(8,128)S(1)} %get-tuple-element.89) | copy-start | bytes 98308
  63.9 266.2 %collective-permute-start.1 = (bf16[384,5,512]{2,0,1:T(8,128)(2,1)}, bf16[384,5,512]{2,0,1:T(8,128)(2,1)}, u32[]{:S(2)}, u32[]{:S(2)}) collective-permute-start(bf16[384,5,512]{2,0,1:T(8,128)(2,1)} %pad_maximum_fusion.4), channel_id=1, source_target_pairs={{0,6},{1,7},{2,0},{3,1},{4,2},{5,3},{6,4},{7,5},{8,14},{9,15},{10,... | collective-permute-start | bytes 5898248 | tf_op jit(solution)/shard_map/ppermute | solution.py:15
  324.5 363.0 %all-to-all-start = ((bf16[4,5,104,1536]{3,2,1,0:T(8,128)(2,1)}), bf16[4,5,104,1536]{3,2,1,0:T(8,128)(2,1)}, u32[]{:S(2)}, u32[]{:S(2)}) async-start(bf16[4,5,104,1536]{3,2,1,0:T(8,128)(2,1)} %bitcast.177), calls=%async_computation | async-start | bytes 12779520 | tf_op jit(solution)/shard_map/all_to_all | solution.py:167
  329.9 484.7 %all-gather.18.cloned.1.call-start = ((), (), s32[]{:S(2)}) async-start(), calls=%async_computation.16 | async-start | bytes 8847360 | tf_op jit(solution)/shard_map/all_gather | solution.py:197
  333.5 339.8 %collective-permute-start.2 = (bf16[768,5,512]{2,0,1:T(8,128)(2,1)}, bf16[768,5,512]{2,0,1:T(8,128)(2,1)}, u32[]{:S(2)}, u32[]{:S(2)}) collective-permute-start(bf16[768,5,512]{2,0,1:T(8,128)(2,1)} %pad_maximum_fusion.1), channel_id=1, source_target_pairs={{0,4},{1,5},{2,6},{3,7},{4,0},{5,1},{6,2},{7,3},{8,12},{9,13},{10,... | collective-permute-start | bytes 11796488 | tf_op jit(solution)/shard_map/ppermute | solution.py:15
  722.4 77.1 %all-to-all-start.1 = ((bf16[4,5,104,1536]{3,2,1,0:T(8,128)(2,1)}), bf16[4,5,104,1536]{3,2,1,0:T(8,128)(2,1)}, u32[]{:S(2)}, u32[]{:S(2)}) async-start(bf16[4,5,104,1536]{3,2,1,0:T(8,128)(2,1)} %copy.89), calls=%async_computation.1 | async-start | bytes 12779520 | tf_op jit(solution)/shard_map/all_to_all | solution.py:173
  804.6 197.1 %copy-start.43 = (bf16[256,20]{0,1:T(8,128)(2,1)}, bf16[256,20]{0,1:T(8,128)(2,1)S(1)}, u32[]{:S(2)}) copy-start(bf16[256,20]{0,1:T(8,128)(2,1)S(1)} %get-tuple-element.59) | copy-start | bytes 30724
  809.3 77.0 %all-to-all-start.2 = ((bf16[4,5,104,1536]{3,2,1,0:T(8,128)(2,1)}), bf16[4,5,104,1536]{3,2,1,0:T(8,128)(2,1)}, u32[]{:S(2)}, u32[]{:S(2)}) async-start(bf16[4,5,104,1536]{3,2,1,0:T(8,128)(2,1)} %bitcast.183), calls=%async_computation.2 | async-start | bytes 12779520 | tf_op jit(solution)/shard_map/all_to_all | solution.py:187
  919.6 77.2 %all-to-all-start.3 = ((bf16[4,5,104,1536]{3,2,1,0:T(8,128)(2,1)}), bf16[4,5,104,1536]{3,2,1,0:T(8,128)(2,1)}, u32[]{:S(2)}, u32[]{:S(2)}) async-start(bf16[4,5,104,1536]{3,2,1,0:T(8,128)(2,1)} %copy.91), calls=%async_computation.3 | async-start | bytes 12779520 | tf_op jit(solution)/shard_map/all_to_all | solution.py:215
  925.1 154.9 %reduce-scatter.18.cloned.1.call-start = ((), (), s32[]{:S(2)}) async-start(), calls=%async_computation.19 | async-start | bytes 1769472 | tf_op jit(solution)/shard_map/reduce_scatter | solution.py:279
  1016.6 131.7 %reduce-scatter.16.cloned.1.call-start = ((), (), s32[]{:S(2)}) async-start(), calls=%async_computation.18 | async-start | bytes 1769472 | tf_op jit(solution)/shard_map/reduce_scatter | solution.py:276
  1029.4 217.0 %reduce-scatter.14.cloned.1.call-start = ((), (), s32[]{:S(2)}) async-start(), calls=%async_computation.17 | async-start | bytes 5308416 | tf_op jit(solution)/shard_map/reduce_scatter | solution.py:273
  1037.2 308.1 %reduce-scatter.20.cloned.1.call-start = ((), (), s32[]{:S(2)}) async-start(), calls=%async_computation.20 | async-start | bytes 5308416 | tf_op jit(solution)/shard_map/reduce_scatter | solution.py:282
  1042.2 368.8 %reduce-scatter.22.cloned.1.call-start = ((), (), s32[]{:S(2)}) async-start(), calls=%async_computation.21 | async-start | bytes 442368
  1044.1 411.6 %all-reduce.10.cloned.1.call-start = ((), (), s32[]{:S(2)}) async-start(), calls=%async_computation.24 | async-start | bytes 3145728 | tf_op jit(solution)/shard_map/psum | solution.py:294
  1345.3 254.1 %reduce-scatter.26.cloned.1.call-start = ((), (), s32[]{:S(2)}) async-start(), calls=%async_computation.23 | async-start | bytes 8847360
  1366.6 486.7 %reduce-scatter.24.cloned.1.call-start = ((), (), s32[]{:S(2)}) async-start(), calls=%async_computation.22 | async-start | bytes 17694720
  (63 other events, 1278.5 us)
Sparse Core Ops, SparseCore 0:
  10.2 61.2 all-gather.7
  73.7 80.8 all-gather.9
  156.8 77.6 all-gather.11
  236.5 77.6 all-gather.13
  316.3 371.6 all-gather.15
  690.1 117.3 all-gather.17
  1016.7 63.1 reduce-scatter.17
  1083.9 64.2 reduce-scatter.15
  1151.9 94.4 reduce-scatter.13
  1249.9 95.3 reduce-scatter.19
  1349.1 61.8 reduce-scatter.21
  1413.4 42.1 all-reduce.9
  1459.2 140.1 reduce-scatter.25
  1602.8 250.3 reduce-scatter.23
